TPU v7x, 128 devices: a whole 4x4x4 slice. The times are simulated.
128 devices in a mesh: section: 2 (over x_hi), seq: 16 (over z, y), mp: 4 (over x_lo, core).
Axes of the slice: x: 4 (x_hi: 2, x_lo: 2; x = x_hi * 2 + x_lo), y: 4, z: 4, core: 2. Of those that a mesh axis runs over, the one named last changes fastest.
Arguments:
- video: bfloat16 [2, 4, 128, 3072], P(None, None, 'seq'), may hold values from -6 to 6
- text: bfloat16 [2, 128, 3072], P(None, 'seq'), may hold values from -6 to 6
- patch_lengths: int32 [2, 4], replicated, may hold values from 1 to 128, 384 in all within a row
- text_len: int32 [2], replicated, may hold values from 64 to 128, as said below
- timestep: int32 [1], replicated, may hold values from 0 to 999
- w_mod: bfloat16 [2, 512, 9216], P('section', None, 'mp'), may hold values from -0.25 to 0.25
- w_qkv: bfloat16 [2, 3072, 3, 3072], P('section', None, None, 'mp')
- w_out: bfloat16 [2, 3072, 3072], P('section', 'mp'), may hold values from -0.109375 to 0.109375
- stale_cache: bfloat16 [2, 2, 4, 128, 2, 3072], P('section', None, None, 'seq', None, 'mp'), may hold values from -6 to 6
Outputs:
- hidden_video: bfloat16 [2, 2, 4, 128, 3072], P('section', None, None, 'seq')
- hidden_text: bfloat16 [2, 2, 128, 3072], P('section', None, 'seq')
- cache_video: bfloat16 [2, 2, 4, 128, 2, 3072], P('section', None, None, 'seq', None, 'mp')
- cache_text: bfloat16 [2, 2, 128, 2, 3072], P('section', None, 'seq', None, 'mp')
Inputs may be any that keep to these rules, and one draw needn't show every extreme that they name: `patch_lengths`: 4 patch lengths per request summing to 384; in every request the largest is 128. `text_len`: exactly one request has 128, every other fewer.
All inputs are finite; a program needn't handle non-finite values.
Results may differ from a plain program's by a relative error of at most 0.01.
Values may be sent and summed in bfloat16 or wider, within the bound.
No kernel may reach another device: no remote copies, remote signals or barrier semaphores. Data moves between devices by JAX's collectives and lax.ppermute only.
A program may use at most 192 MiB of HBM per device.

v0:
```python
import math
import jax
import jax.numpy as jnp
from jax import lax
from jax.sharding import PartitionSpec as P

HEAD = 64
EPS = 1e-05
NEG = -1e30


def passed_along(value, axis, steps):
    count = lax.axis_size(axis)
    leading, last = (max(0, -steps), min(count, count - steps))
    return lax.ppermute(value, axis, [(source, source + steps) for source in range(leading, last)])


def modulation(timestep, weight):
    half_width = weight.shape[0] // 2
    frequency = jnp.exp(-math.log(10000.0) * jnp.arange(half_width, dtype=jnp.float32) / half_width)
    phases = timestep.astype(jnp.float32)[0] * frequency
    embedding = jnp.concatenate([jnp.cos(phases), jnp.sin(phases)])
    active = jax.nn.silu(embedding).astype(jnp.bfloat16)
    return jnp.dot(active[None, :], weight, preferred_element_type=jnp.float32)[0]


def normalize(token_rows, shift_vec, scale_vec):
    values = token_rows.astype(jnp.float32)
    center = values - jnp.mean(values, axis=-1, keepdims=True)
    spread = jnp.mean(center * center, axis=-1, keepdims=True)
    return (center * lax.rsqrt(spread + EPS) * (1.0 + scale_vec) + shift_vec).astype(jnp.bfloat16)


def scores_of(query_heads, key_value, head_count):
    requests, key_count = (key_value.shape[0], key_value.shape[1])
    key_heads = key_value[:, :, 0].reshape(requests, key_count, head_count, HEAD)
    value_heads = key_value[:, :, 1].reshape(requests, key_count, head_count, HEAD)
    scores = jnp.einsum(
        "rqhe,rkhe->rhqk", query_heads, key_heads, preferred_element_type=jnp.float32
    ) * HEAD ** (-0.5)
    return (scores, value_heads)


def masked_max(scores, key_mask):
    return jnp.max(jnp.where(key_mask[:, None, None, :], scores, NEG), axis=-1)


def weighed(scores, key_mask, top_score, value_heads):
    weights = jnp.where(key_mask[:, None, None, :], jnp.exp(scores - top_score[..., None]), 0.0)
    weight_sum = jnp.sum(weights, axis=-1)
    accumulated = jnp.einsum(
        "rhqk,rkhe->rhqe",
        weights.astype(jnp.bfloat16),
        value_heads,
        preferred_element_type=jnp.float32,
    )
    return (weight_sum, accumulated)


def body(video, text, patch_lengths, text_len, timestep, w_mod, w_qkv, w_out, stale_cache):
    section_index = lax.axis_index("section")
    seq_count = lax.axis_size("seq")
    requests, patches, per_dev, model_width = video.shape
    text_dev = text.shape[1]
    capacity = per_dev * seq_count
    text_slots = text_dev * seq_count
    column_count = w_out.shape[1]
    head_count = column_count // HEAD
    row_count = per_dev + text_dev
    modulated = lax.all_gather(modulation(timestep, w_mod[0]), "mp", axis=0, tiled=True)
    shift_vec = modulated[:model_width]
    scale_vec = modulated[model_width : 2 * model_width]
    gate_vec = modulated[2 * model_width :]
    weight_qkv = w_qkv[0].reshape(model_width, 3 * column_count)
    weight_out = w_out[0]
    stale_local = stale_cache[0]
    slot_index = jnp.arange(capacity, dtype=jnp.int32)
    video_valid = (slot_index[None, None, :] < patch_lengths[:, :, None]).reshape(requests, -1)
    text_valid = jnp.arange(text_slots, dtype=jnp.int32)[None, :] < text_len[:, None]
    all_valid = jnp.concatenate([video_valid, text_valid], axis=1)
    video_patch = jnp.repeat(jnp.arange(patches, dtype=jnp.int32), capacity)
    all_patch = jnp.concatenate([video_patch, jnp.zeros((text_slots,), jnp.int32)])
    stale_whole = lax.all_gather(stale_local, "seq", axis=2, tiled=True).reshape(
        requests, patches * capacity, 2, column_count
    )
    fresh_video = jnp.zeros((requests, patches, capacity, 2, column_count), jnp.bfloat16)
    fresh_text = jnp.zeros((requests, text_slots, 2, column_count), jnp.bfloat16)
    own_video = jnp.zeros((requests, patches, per_dev, 2, column_count), jnp.bfloat16)
    own_text = jnp.zeros((requests, text_dev, 2, column_count), jnp.bfloat16)
    out_video = jnp.zeros((requests, patches, per_dev, model_width), jnp.bfloat16)
    out_text = jnp.zeros((requests, text_dev, model_width), jnp.bfloat16)
    received = jnp.zeros((requests, row_count, model_width), jnp.bfloat16)
    patch_ids = jnp.arange(patches, dtype=jnp.int32)
    for turn_index in range(patches + 1):
        patch_now = turn_index - section_index
        picked = lax.dynamic_index_in_dim(
            video, jnp.clip(patch_now, 0, patches - 1), 1, keepdims=False
        )
        token_rows = jnp.where(
            section_index == 0, jnp.concatenate([picked, text], axis=1), received
        )
        normed = normalize(token_rows, shift_vec, scale_vec)
        projected = jnp.dot(
            normed.reshape(-1, model_width), weight_qkv, preferred_element_type=jnp.float32
        )
        projected = projected.reshape(requests, row_count, 3, column_count).astype(jnp.bfloat16)
        queries = projected[:, :, 0]
        key_value = projected[:, :, 1:]
        gathered_video, gathered_text = (
            lax.all_gather(key_value[:, :per_dev], "seq", axis=1, tiled=True),
            lax.all_gather(key_value[:, per_dev:], "seq", axis=1, tiled=True),
        )
        current = patch_ids == patch_now
        fresh_video = jnp.where(
            current[None, :, None, None, None], gathered_video[:, None], fresh_video
        )
        fresh_text = jnp.where(patch_now == 0, gathered_text, fresh_text)
        own_video = jnp.where(
            current[None, :, None, None, None], key_value[:, None, :per_dev], own_video
        )
        own_text = jnp.where(patch_now == 0, key_value[:, per_dev:], own_text)
        fresh_all = jnp.concatenate(
            [fresh_video.reshape(requests, patches * capacity, 2, column_count), fresh_text], axis=1
        )
        fresh_mask = all_valid & (all_patch[None, :] <= patch_now)
        query_heads = queries.reshape(requests, row_count, head_count, HEAD)
        scores, value_heads = scores_of(query_heads, fresh_all, head_count)
        fresh_top = masked_max(scores, fresh_mask)
        fresh_sum, fresh_acc = weighed(scores, fresh_mask, fresh_top, value_heads)
        stale_mask = video_valid & (video_patch[None, :] > patch_now)
        scores, value_heads = scores_of(query_heads, stale_whole, head_count)
        stale_top = masked_max(scores, stale_mask)
        stale_sum, stale_acc = weighed(scores, stale_mask, stale_top, value_heads)
        top_score = jnp.maximum(fresh_top, stale_top)
        fresh_weight = jnp.exp(fresh_top - top_score)
        stale_weight = jnp.exp(stale_top - top_score)
        numer = fresh_acc * fresh_weight[..., None] + stale_acc * stale_weight[..., None]
        denom = fresh_sum * fresh_weight + stale_sum * stale_weight
        attended = (numer / denom[..., None]).astype(jnp.bfloat16)
        attended = attended.transpose(0, 2, 1, 3).reshape(requests * row_count, column_count)
        partial_out = jnp.dot(attended, weight_out, preferred_element_type=jnp.float32).reshape(
            requests, row_count, model_width
        )
        summed = lax.psum(partial_out, "mp")
        result = (token_rows.astype(jnp.float32) + gate_vec * summed).astype(jnp.bfloat16)
        out_video = jnp.where(current[None, :, None, None], result[:, None, :per_dev], out_video)
        out_text = jnp.where(patch_now == 0, result[:, per_dev:], out_text)
        if turn_index < patches:
            received = passed_along(result, "section", 1)
    return (out_video[None], out_text[None], own_video[None], own_text[None])


def solution(mesh):
    placed = (
        P(None, None, "seq", None),
        P(None, "seq", None),
        P(),
        P(),
        P(),
        P("section", None, "mp"),
        P("section", None, None, "mp"),
        P("section", "mp", None),
        P("section", None, None, "seq", None, "mp"),
    )
    return jax.shard_map(
        body,
        mesh=mesh,
        in_specs=placed,
        out_specs=(
            P("section", None, None, "seq", None),
            P("section", None, "seq", None),
            P("section", None, None, "seq", None, "mp"),
            P("section", None, "seq", None, "mp"),
        ),
        check_vma=False,
    )
```

profile of v0, /device:TPU:1, one launch (start us, length us, event | category | flops | bytes accessed | tf_op | source)
XLA Modules:
  0.0 716.3 jit_solution(2597853420989053191)
XLA Ops:
  8.0 18.7 %copy.75 = bf16[1,3072,3,768]{1,3,2,0:T(8,128)(2,1)} copy(bf16[1,3072,3,768]{3,1,2,0:T(8,128)(2,1)} %param.15) | data formatting | bytes 28311552 | tf_op args[6]
  27.8 6.4 all-gather.1
  35.4 9.3 %fusion.26 = bf16[2,16,3,768]{3,1,2,0:T(8,128)(2,1)S(1)} fusion(bf16[1,3072,3,768]{1,3,2,0:T(8,128)(2,1)} %copy.75, f32[3072]{0:T(1024)S(1)} %get-tuple-element.76, f32[3072]{0:T(1024)S(1)} %get-tuple-element.77, f32[2,16]{1,0:T(2,128)S(1)} %add_rsqrt_fusion.4, f32[2,16]{1,0:T(2,128)S(1)} %broadcast_multiply_fusion.4, ...), kind=kOutput, calls=%fused_computation.57 | convolution fusion | flops 454139904 | bytes 14524673 | tf_op jit(solution)/shard_map/dot_general | solution.py:103
  44.9 24.0 %all_gather.38 = bf16[2,128,2,768]{3,1,2,0:T(8,128)(2,1)S(1)} all-gather(bf16[2,8,2,768]{3,1,2,0:T(8,128)(2,1)S(1)} %get-tuple-element.73), channel_id=1, replica_groups=mesh['section'=2,'seq'=16,'mp'=4] {'seq'}, dimensions={1}, use_global_device_ids=true | all-gather | bytes 835584 | tf_op jit(solution)/shard_map/all_gather | solution.py:111
  70.1 17.7 %all_gather.37 = bf16[2,128,2,768]{3,1,2,0:T(8,128)(2,1)S(1)} all-gather(bf16[2,8,2,768]{3,1,2,0:T(8,128)(2,1)S(1)} %get-tuple-element.74), channel_id=1, replica_groups=mesh['section'=2,'seq'=16,'mp'=4] {'seq'}, dimensions={1}, use_global_device_ids=true | all-gather | bytes 835584 | tf_op jit(solution)/shard_map/all_gather | solution.py:110
  88.1 2.5 broadcast_in_dim.474
  90.6 5.7 broadcast_in_dim.475
  96.5 2.2 broadcast_select_fusion.4
  98.8 1.5 pad_maximum_fusion.4
  102.9 9.3 %fusion.259 = (bf16[2,512,1,768]{3,2,1,0:T(2,128)(2,1)}, bf16[2,512,1,768]{3,2,1,0:T(2,128)(2,1)}) fusion(bf16[2,512,2,768]{3,2,1,0:T(2,128)(2,1)} %bitcast.353), kind=kLoop, calls=%fused_computation.383 | loop fusion | bytes 6291456 | tf_op jit(solution)/shard_map/slice | solution.py:36
  112.2 6.8 copy.115
  119.0 8.1 %copy.114 = bf16[2,512,1,768]{1,3,0,2:T(8,128)(2,1)} copy(bf16[2,512,1,768]{3,2,1,0:T(2,128)(2,1)} %get-tuple-element.51) | data formatting | bytes 3145728
  127.1 2.0 select_reduce_fusion.9
  131.0 4.0 fusion.18
  135.2 45.4 %all-reduce.7.cloned.1.call-done = f32[2,16,3072]{2,1,0:T(8,128)} async-done(((f32[2,16,3072]{2,1,0:T(8,128)}), f32[2,16,3072]{2,1,0:T(8,128)}) %all-reduce.7.cloned.1.call-update) | async-done | bytes 393232 | tf_op jit(solution)/shard_map/psum | solution.py:144
  181.7 4.3 collective-permute-start
  186.6 3.5 collective-permute-done
  190.5 9.3 %fusion.29 = bf16[2,16,3,768]{3,1,2,0:T(8,128)(2,1)S(1)} fusion(bf16[1,3072,3,768]{1,3,2,0:T(8,128)(2,1)} %copy.75, bf16[2,16,3072]{2,1,0:T(8,128)(2,1)S(1)} %get-tuple-element.37, f32[2,16]{1,0:T(2,128)S(1)} %add_rsqrt_fusion.3, f32[2,16]{1,0:T(2,128)S(1)} %broadcast_multiply_fusion.3, f32[3072]{0:T(1024)S(1)} %get-tuple-element.76, ...), kind=kOutput, calls=%fused_computation.58 | convolution fusion | flops 453648384 | bytes 14524672 | tf_op jit(solution)/shard_map/dot_general | solution.py:103
  201.3 19.7 %all_gather.41 = bf16[2,128,2,768]{3,1,2,0:T(8,128)(2,1)S(1)} all-gather(bf16[2,8,2,768]{3,1,2,0:T(8,128)(2,1)S(1)} %get-tuple-element.71), channel_id=1, replica_groups=mesh['section'=2,'seq'=16,'mp'=4] {'seq'}, dimensions={1}, use_global_device_ids=true | all-gather | bytes 835584 | tf_op jit(solution)/shard_map/all_gather | solution.py:111
  221.1 1.2 copy.84
  222.3 19.1 %all_gather.40 = bf16[2,128,2,768]{3,1,2,0:T(8,128)(2,1)S(1)} all-gather(bf16[2,8,2,768]{3,1,2,0:T(8,128)(2,1)} %get-tuple-element.72), channel_id=1, replica_groups=mesh['section'=2,'seq'=16,'mp'=4] {'seq'}, dimensions={1}, use_global_device_ids=true | all-gather | bytes 835584 | tf_op jit(solution)/shard_map/all_gather | solution.py:110
  242.6 3.6 broadcast_in_dim.487
  246.2 5.8 broadcast_in_dim.488
  252.0 2.0 select_reduce_fusion.8
  254.3 2.4 broadcast_select_fusion.3
  260.8 4.0 fusion.16
  264.9 47.4 %all-reduce.9.cloned.1.call-done = f32[2,16,3072]{2,1,0:T(8,128)} async-done(((f32[2,16,3072]{2,1,0:T(8,128)}), f32[2,16,3072]{2,1,0:T(8,128)}) %all-reduce.9.cloned.1.call-update) | async-done | bytes 393232 | tf_op jit(solution)/shard_map/psum | solution.py:144
  313.4 4.3 collective-permute-start.1
  318.3 3.5 collective-permute-done.1
  322.2 9.3 %fusion.32 = bf16[2,16,3,768]{3,1,2,0:T(8,128)(2,1)S(1)} fusion(bf16[1,3072,3,768]{1,3,2,0:T(8,128)(2,1)} %copy.75, bf16[2,16,3072]{2,1,0:T(8,128)(2,1)S(1)} %get-tuple-element.32, f32[2,16]{1,0:T(2,128)S(1)} %add_rsqrt_fusion.2, f32[2,16]{1,0:T(2,128)S(1)} %broadcast_multiply_fusion.2, f32[3072]{0:T(1024)S(1)} %get-tuple-element.76, ...), kind=kOutput, calls=%fused_computation.59 | convolution fusion | flops 453648384 | bytes 14524672 | tf_op jit(solution)/shard_map/dot_general | solution.py:103
  333.6 19.7 %all_gather.43 = bf16[2,128,2,768]{3,1,2,0:T(8,128)(2,1)S(1)} all-gather(bf16[2,8,2,768]{3,1,2,0:T(8,128)(2,1)S(1)} %get-tuple-element.69), channel_id=1, replica_groups=mesh['section'=2,'seq'=16,'mp'=4] {'seq'}, dimensions={1}, use_global_device_ids=true | all-gather | bytes 835584 | tf_op jit(solution)/shard_map/all_gather | solution.py:111
  353.4 1.2 copy.89
  354.6 19.2 %all_gather.42 = bf16[2,128,2,768]{3,1,2,0:T(8,128)(2,1)S(1)} all-gather(bf16[2,8,2,768]{3,1,2,0:T(8,128)(2,1)} %get-tuple-element.70), channel_id=1, replica_groups=mesh['section'=2,'seq'=16,'mp'=4] {'seq'}, dimensions={1}, use_global_device_ids=true | all-gather | bytes 835584 | tf_op jit(solution)/shard_map/all_gather | solution.py:110
  374.9 3.6 broadcast_in_dim.494
  378.5 5.7 broadcast_in_dim.495
  384.2 2.0 select_reduce_fusion.7
  386.7 2.4 broadcast_select_fusion.2
  393.1 4.0 fusion.14
  397.2 47.5 %all-reduce.11.cloned.1.call-done = f32[2,16,3072]{2,1,0:T(8,128)} async-done(((f32[2,16,3072]{2,1,0:T(8,128)}), f32[2,16,3072]{2,1,0:T(8,128)}) %all-reduce.11.cloned.1.call-update) | async-done | bytes 393232 | tf_op jit(solution)/shard_map/psum | solution.py:144
  445.8 4.3 collective-permute-start.2
  450.8 3.5 collective-permute-done.2
  454.6 9.3 %fusion.35 = bf16[2,16,3,768]{3,1,2,0:T(8,128)(2,1)S(1)} fusion(bf16[1,3072,3,768]{1,3,2,0:T(8,128)(2,1)} %copy.75, bf16[2,16,3072]{2,1,0:T(8,128)(2,1)S(1)} %get-tuple-element.27, f32[2,16]{1,0:T(2,128)S(1)} %add_rsqrt_fusion.1, f32[2,16]{1,0:T(2,128)S(1)} %broadcast_multiply_fusion.1, f32[3072]{0:T(1024)S(1)} %get-tuple-element.76, ...), kind=kOutput, calls=%fused_computation.60 | convolution fusion | flops 453648384 | bytes 14524672 | tf_op jit(solution)/shard_map/dot_general | solution.py:103
  465.4 19.7 %all_gather.45 = bf16[2,128,2,768]{3,1,2,0:T(8,128)(2,1)S(1)} all-gather(bf16[2,8,2,768]{3,1,2,0:T(8,128)(2,1)S(1)} %get-tuple-element.67), channel_id=1, replica_groups=mesh['section'=2,'seq'=16,'mp'=4] {'seq'}, dimensions={1}, use_global_device_ids=true | all-gather | bytes 835584 | tf_op jit(solution)/shard_map/all_gather | solution.py:111
  485.2 1.2 copy.94
  486.4 19.2 %all_gather.44 = bf16[2,128,2,768]{3,1,2,0:T(8,128)(2,1)S(1)} all-gather(bf16[2,8,2,768]{3,1,2,0:T(8,128)(2,1)} %get-tuple-element.68), channel_id=1, replica_groups=mesh['section'=2,'seq'=16,'mp'=4] {'seq'}, dimensions={1}, use_global_device_ids=true | all-gather | bytes 835584 | tf_op jit(solution)/shard_map/all_gather | solution.py:110
  506.8 3.6 broadcast_in_dim.501
  510.4 5.8 broadcast_in_dim.502
  516.2 2.0 select_reduce_fusion.6
  518.5 2.4 broadcast_select_fusion.1
  525.0 4.0 fusion.12
  529.1 47.4 %all-reduce.13.cloned.1.call-done = f32[2,16,3072]{2,1,0:T(8,128)} async-done(((f32[2,16,3072]{2,1,0:T(8,128)}), f32[2,16,3072]{2,1,0:T(8,128)}) %all-reduce.13.cloned.1.call-update) | async-done | bytes 393232 | tf_op jit(solution)/shard_map/psum | solution.py:144
  577.6 4.3 collective-permute-start.3
  582.5 3.5 collective-permute-done.3
  586.4 9.3 %fusion.38 = bf16[2,16,3,768]{3,1,2,0:T(8,128)(2,1)S(1)} fusion(bf16[1,3072,3,768]{1,3,2,0:T(8,128)(2,1)} %copy.75, bf16[2,16,3072]{2,1,0:T(8,128)(2,1)S(1)} %get-tuple-element.22, f32[2,16]{1,0:T(2,128)S(1)} %add_rsqrt_fusion, f32[2,16]{1,0:T(2,128)S(1)} %broadcast_multiply_fusion, f32[3072]{0:T(1024)S(1)} %get-tuple-element.76, ...), kind=kOutput, calls=%fused_computation.61 | convolution fusion | flops 453648384 | bytes 14524672 | tf_op jit(solution)/shard_map/dot_general | solution.py:103
  595.9 1.5 select_bitcast_fusion
  597.4 19.7 %all_gather.47 = bf16[2,128,2,768]{3,1,2,0:T(8,128)(2,1)S(1)} all-gather(bf16[2,8,2,768]{3,1,2,0:T(8,128)(2,1)S(1)} %get-tuple-element.65), channel_id=1, replica_groups=mesh['section'=2,'seq'=16,'mp'=4] {'seq'}, dimensions={1}, use_global_device_ids=true | all-gather | bytes 835584 | tf_op jit(solution)/shard_map/all_gather | solution.py:111
  618.3 19.2 %all_gather.46 = bf16[2,128,2,768]{3,1,2,0:T(8,128)(2,1)S(1)} all-gather(bf16[2,8,2,768]{3,1,2,0:T(8,128)(2,1)} %get-tuple-element.66), channel_id=1, replica_groups=mesh['section'=2,'seq'=16,'mp'=4] {'seq'}, dimensions={1}, use_global_device_ids=true | all-gather | bytes 835584 | tf_op jit(solution)/shard_map/all_gather | solution.py:110
  637.9 2.5 broadcast_in_dim.508
  640.4 5.7 broadcast_in_dim.509
  646.2 2.0 select_reduce_fusion.5
  648.5 2.4 broadcast_select_fusion
  654.4 4.2 fusion.10
  660.5 1.5 copy.108
  663.0 43.2 %all-reduce.15.cloned.1.call-done = f32[2,16,3072]{2,1,0:T(8,128)} async-done(((f32[2,16,3072]{2,1,0:T(8,128)}), f32[2,16,3072]{2,1,0:T(8,128)}) %all-reduce.15.cloned.1.call-update) | async-done | bytes 393232 | tf_op jit(solution)/shard_map/psum | solution.py:144
  (255 shorter events, 50.0 us)
Async XLA Ops:
  7.2 20.3 %copy-start = (bf16[1,512,2304]{2,1,0:T(8,128)(2,1)S(1)}, bf16[1,512,2304]{2,1,0:T(8,128)(2,1)}, u32[]{:S(2)}) copy-start(bf16[1,512,2304]{2,1,0:T(8,128)(2,1)} %param.14) | copy-start | bytes 7077892
  7.2 95.7 %all-gather.4.cloned.1.call-start = ((), (), s32[]{:S(2)}) async-start(), calls=%async_computation.5 | async-start | bytes 3342336 | tf_op jit(solution)/shard_map/all_gather | solution.py:83
  7.9 172.7 %all-reduce.7.cloned.1.call-start = ((), (), s32[]{:S(2)}) async-start(), calls=%async_computation | async-start | bytes 786432 | tf_op jit(solution)/shard_map/psum | solution.py:144
  8.0 26.3 %copy-start.34 = (bf16[2,4,8,3072]{3,2,1,0:T(8,128)(2,1)S(1)}, bf16[2,4,8,3072]{3,2,1,0:T(8,128)(2,1)}, u32[]{:S(2)}) copy-start(bf16[2,4,8,3072]{3,2,1,0:T(8,128)(2,1)} %param.9) | copy-start | bytes 1179652
  26.6 8.4 %copy-start.9 = (bf16[2,8,3072]{2,1,0:T(8,128)(2,1)S(1)}, bf16[2,8,3072]{2,1,0:T(8,128)(2,1)}, u32[]{:S(2)}) copy-start(bf16[2,8,3072]{2,1,0:T(8,128)(2,1)} %param.10) | copy-start | bytes 294916
  44.7 43.5 %copy-start.22 = (bf16[2,16,3,768]{3,1,2,0:T(8,128)(2,1)}, bf16[2,16,3,768]{3,1,2,0:T(8,128)(2,1)S(1)}, u32[]{:S(2)}) copy-start(bf16[2,16,3,768]{3,1,2,0:T(8,128)(2,1)S(1)} %fusion.26) | copy-start | bytes 442372
  44.9 56.1 %copy-start.18 = (bf16[2,16,12,64]{3,2,1,0:T(8,128)(2,1)}, bf16[2,16,12,64]{3,2,1,0:T(8,128)(2,1)S(1)}, u32[]{:S(2)}) copy-start(bf16[2,16,12,64]{3,2,1,0:T(8,128)(2,1)S(1)} %reshape_squeeze.63) | copy-start | bytes 147460
  96.4 2.3 copy-start.44
  96.5 2.2 copy-start.42
  96.5 2.2 copy-start.12
  98.7 1.5 copy-start.55
  98.8 1.6 copy-start.50
  127.1 2.9 copy-start.11
  127.1 2.9 copy-start.17
  131.0 59.1 %copy-start.40 = (bf16[2,8,3072]{2,1,0:T(8,128)(2,1)S(1)}, bf16[2,8,3072]{2,1,0:T(8,128)(2,1)}, u32[]{:S(2)}) copy-start(bf16[2,8,3072]{2,1,0:T(8,128)(2,1)} %get-tuple-element.57) | copy-start | bytes 294916
  135.1 177.3 %all-reduce.9.cloned.1.call-start = ((), (), s32[]{:S(2)}) async-start(), calls=%async_computation.1 | async-start | bytes 786432 | tf_op jit(solution)/shard_map/psum | solution.py:144
  135.2 55.0 %copy-start.46 = (pred[4]{0:T(512)(128)(4,1)}, pred[4]{0:T(512)(128)(4,1)S(1)}, u32[]{:S(2)}) copy-start(pred[4]{0:T(512)(128)(4,1)S(1)} %iota_compare_fusion.3) | copy-start | bytes 16
  181.7 8.8 %copy-start.26 = (bf16[2,16,3072]{2,1,0:T(8,128)(2,1)}, bf16[2,16,3072]{2,1,0:T(8,128)(2,1)S(1)}, u32[]{:S(2)}) copy-start(bf16[2,16,3072]{2,1,0:T(8,128)(2,1)S(1)} %fusion.136) | copy-start | bytes 589828
  181.7 8.4 %collective-permute-start = (bf16[2,16,3072]{2,1,0:T(8,128)(2,1)S(1)}, bf16[2,16,3072]{2,1,0:T(8,128)(2,1)S(1)}, u32[]{:S(2)}, u32[]{:S(2)}) collective-permute-start(bf16[2,16,3072]{2,1,0:T(8,128)(2,1)S(1)} %fusion.136), channel_id=1, source_target_pairs={{0,64},{1,65},{2,66},{3,67},{4,68},{5,69},{6,70},{7,71},{8,72},{9,... | collective-permute-start | bytes 589832 | tf_op jit(solution)/shard_map/ppermute | solution.py:15
  199.8 1.5 copy-start.23
  246.2 5.8 copy-start.19
  252.0 2.4 copy-start.2
  252.0 2.4 copy-start.43
  252.0 2.4 copy-start.52
  254.3 2.4 copy-start.14
  256.7 1.6 copy-start.3
  256.7 1.6 copy-start.41
  260.8 61.1 %copy-start.39 = (bf16[2,8,3072]{2,1,0:T(8,128)(2,1)S(1)}, bf16[2,8,3072]{2,1,0:T(8,128)(2,1)}, u32[]{:S(2)}) copy-start(bf16[2,8,3072]{2,1,0:T(8,128)(2,1)} %get-tuple-element.54) | copy-start | bytes 294916
  264.8 179.9 %all-reduce.11.cloned.1.call-start = ((), (), s32[]{:S(2)}) async-start(), calls=%async_computation.2 | async-start | bytes 786432 | tf_op jit(solution)/shard_map/psum | solution.py:144
  264.9 57.1 %copy-start.48 = (pred[4]{0:T(512)(128)(4,1)}, pred[4]{0:T(512)(128)(4,1)S(1)}, u32[]{:S(2)}) copy-start(pred[4]{0:T(512)(128)(4,1)S(1)} %iota_compare_fusion.2) | copy-start | bytes 16
  313.4 8.8 %copy-start.28 = (bf16[2,16,3072]{2,1,0:T(8,128)(2,1)}, bf16[2,16,3072]{2,1,0:T(8,128)(2,1)S(1)}, u32[]{:S(2)}) copy-start(bf16[2,16,3072]{2,1,0:T(8,128)(2,1)S(1)} %fusion.137) | copy-start | bytes 589828
  313.4 8.4 %collective-permute-start.1 = (bf16[2,16,3072]{2,1,0:T(8,128)(2,1)S(1)}, bf16[2,16,3072]{2,1,0:T(8,128)(2,1)S(1)}, u32[]{:S(2)}, u32[]{:S(2)}) collective-permute-start(bf16[2,16,3072]{2,1,0:T(8,128)(2,1)S(1)} %fusion.137), channel_id=1, source_target_pairs={{0,64},{1,65},{2,66},{3,67},{4,68},{5,69},{6,70},{7,71},{8,72},{9,... | collective-permute-start | bytes 589832 | tf_op jit(solution)/shard_map/ppermute | solution.py:15
  384.2 2.4 copy-start.4
  384.2 2.4 copy-start.54
  386.7 2.4 copy-start.16
  389.1 1.6 copy-start.7
  389.1 1.6 copy-start.21
  393.1 61.2 %copy-start.38 = (bf16[2,8,3072]{2,1,0:T(8,128)(2,1)S(1)}, bf16[2,8,3072]{2,1,0:T(8,128)(2,1)}, u32[]{:S(2)}) copy-start(bf16[2,8,3072]{2,1,0:T(8,128)(2,1)} %get-tuple-element.55) | copy-start | bytes 294916
  397.1 179.4 %all-reduce.13.cloned.1.call-start = ((), (), s32[]{:S(2)}) async-start(), calls=%async_computation.3 | async-start | bytes 786432 | tf_op jit(solution)/shard_map/psum | solution.py:144
  445.8 8.8 %copy-start.30 = (bf16[2,16,3072]{2,1,0:T(8,128)(2,1)}, bf16[2,16,3072]{2,1,0:T(8,128)(2,1)S(1)}, u32[]{:S(2)}) copy-start(bf16[2,16,3072]{2,1,0:T(8,128)(2,1)S(1)} %fusion.138) | copy-start | bytes 589828
  445.8 8.4 %collective-permute-start.2 = (bf16[2,16,3072]{2,1,0:T(8,128)(2,1)S(1)}, bf16[2,16,3072]{2,1,0:T(8,128)(2,1)S(1)}, u32[]{:S(2)}, u32[]{:S(2)}) collective-permute-start(bf16[2,16,3072]{2,1,0:T(8,128)(2,1)S(1)} %fusion.138), channel_id=1, source_target_pairs={{0,64},{1,65},{2,66},{3,67},{4,68},{5,69},{6,70},{7,71},{8,72},{9,... | collective-permute-start | bytes 589832 | tf_op jit(solution)/shard_map/ppermute | solution.py:15
  463.9 1.5 copy-start.25
  510.4 5.8 copy-start.20
  516.2 2.4 copy-start.8
  516.2 2.4 copy-start.53
  518.5 2.4 copy-start.15
  520.9 1.6 copy-start.5
  524.9 61.1 %copy-start.37 = (bf16[2,8,3072]{2,1,0:T(8,128)(2,1)S(1)}, bf16[2,8,3072]{2,1,0:T(8,128)(2,1)}, u32[]{:S(2)}) copy-start(bf16[2,8,3072]{2,1,0:T(8,128)(2,1)} %get-tuple-element.53) | copy-start | bytes 294916
  529.0 177.2 %all-reduce.15.cloned.1.call-start = ((), (), s32[]{:S(2)}) async-start(), calls=%async_computation.4 | async-start | bytes 786432 | tf_op jit(solution)/shard_map/psum | solution.py:144
  577.6 8.6 %copy-start.32 = (bf16[2,16,3072]{2,1,0:T(8,128)(2,1)}, bf16[2,16,3072]{2,1,0:T(8,128)(2,1)S(1)}, u32[]{:S(2)}) copy-start(bf16[2,16,3072]{2,1,0:T(8,128)(2,1)S(1)} %fusion.139) | copy-start | bytes 589828
  577.6 8.4 %collective-permute-start.3 = (bf16[2,16,3072]{2,1,0:T(8,128)(2,1)S(1)}, bf16[2,16,3072]{2,1,0:T(8,128)(2,1)S(1)}, u32[]{:S(2)}, u32[]{:S(2)}) collective-permute-start(bf16[2,16,3072]{2,1,0:T(8,128)(2,1)S(1)} %fusion.139), channel_id=1, source_target_pairs={{0,64},{1,65},{2,66},{3,67},{4,68},{5,69},{6,70},{7,71},{8,72},{9,... | collective-permute-start | bytes 589832 | tf_op jit(solution)/shard_map/ppermute | solution.py:15
  646.2 2.4 copy-start.6
  646.2 2.4 copy-start.51
  648.5 2.4 copy-start.13
  654.4 4.3 copy-start.35
  654.4 4.4 copy-start.36
  654.4 7.6 %copy-start.45 = (pred[4]{0:T(512)(128)(4,1)S(1)}, pred[4]{0:T(512)(128)(4,1)}, u32[]{:S(2)}) copy-start(pred[4]{0:T(512)(128)(4,1)} %copy-done.44) | copy-start | bytes 16
  654.4 7.6 %copy-start.47 = (pred[4]{0:T(512)(128)(4,1)S(1)}, pred[4]{0:T(512)(128)(4,1)}, u32[]{:S(2)}) copy-start(pred[4]{0:T(512)(128)(4,1)} %copy-done.46) | copy-start | bytes 16
  654.4 7.6 %copy-start.49 = (pred[4]{0:T(512)(128)(4,1)S(1)}, pred[4]{0:T(512)(128)(4,1)}, u32[]{:S(2)}) copy-start(pred[4]{0:T(512)(128)(4,1)} %copy-done.48) | copy-start | bytes 16
  654.4 52.9 %copy-start.27 = (bf16[2,16,3072]{2,1,0:T(8,128)(2,1)S(1)}, bf16[2,16,3072]{2,1,0:T(8,128)(2,1)}, u32[]{:S(2)}) copy-start(bf16[2,16,3072]{2,1,0:T(8,128)(2,1)} %copy-done.26) | copy-start | bytes 589828
  654.4 52.9 %copy-start.29 = (bf16[2,16,3072]{2,1,0:T(8,128)(2,1)S(1)}, bf16[2,16,3072]{2,1,0:T(8,128)(2,1)}, u32[]{:S(2)}) copy-start(bf16[2,16,3072]{2,1,0:T(8,128)(2,1)} %copy-done.28) | copy-start | bytes 589828
  654.4 52.9 %copy-start.31 = (bf16[2,16,3072]{2,1,0:T(8,128)(2,1)S(1)}, bf16[2,16,3072]{2,1,0:T(8,128)(2,1)}, u32[]{:S(2)}) copy-start(bf16[2,16,3072]{2,1,0:T(8,128)(2,1)} %copy-done.30) | copy-start | bytes 589828
  654.4 52.9 %copy-start.33 = (bf16[2,16,3072]{2,1,0:T(8,128)(2,1)S(1)}, bf16[2,16,3072]{2,1,0:T(8,128)(2,1)}, u32[]{:S(2)}) copy-start(bf16[2,16,3072]{2,1,0:T(8,128)(2,1)} %copy-done.32) | copy-start | bytes 589828
  654.4 54.5 %copy-start.1 = (bf16[1,512,2304]{2,1,0:T(8,128)(2,1)S(1)}, bf16[1,512,2304]{2,1,0:T(8,128)(2,1)}, u32[]{:S(2)}) copy-start(bf16[1,512,2304]{2,1,0:T(8,128)(2,1)} %param.14) | copy-start | bytes 7077892
  (2 other events, 1.7 us)
Sparse Core Ops, SparseCore 0:
  10.2 52.0 all-gather.3
  135.2 45.3 all-reduce.6
  264.9 47.3 all-reduce.8
  397.3 47.4 all-reduce.10
  529.1 47.3 all-reduce.12
  658.8 47.4 all-reduce.14
where the time goes:
time: 723 us; the launch traced here: 716 us
  waiting for transfers between devices  246 us (34%)
  blocking collectives  203 us (28%)
  local copies, waits for them, and re-layouts  116 us (16%)
  matrix products  86.7 us (12%)
  other arithmetic  30.2 us (4%)
  starting transfers between devices  17.5 us (2%)
  between operations  16.3 us (2%)
    psum x5, waiting for transfers between devices, body(): summed = lax.psum(partial_out, 'mp')  231 us
    all_gather x5, blocking collectives, body(): lax.all_gather(key_value[:, per_dev:], 'seq', axis=1, tiled=True)  103 us
    all_gather x5, blocking collectives, body(): lax.all_gather(key_value[:, :per_dev], 'seq', axis=1, tiled=True)  94.4 us
    broadcast_in_dim x15, local copies, waits for them, and re-layouts, body(): jnp.where(current[None, :, None, None, None], gathered_video[:, None], fr...  47 us
    dot_general x5, matrix products, body(): jnp.dot(normed.reshape(-1, model_width), weight_qkv, preferred_element_ty...  46.6 us
    unnamed x117, local copies, waits for them, and re-layouts  41 us
    dot_general x5, matrix products, body(): jnp.dot(attended, weight_out, preferred_element_type=jnp.float32)  20.3 us
    ppermute x4, starting transfers between devices, passed_along(): lax.ppermute(value, axis, [(source, source + steps) for source in range(l...  17.3 us
  transfers between devices with their start and end apart: 10, of which 9 were waited for; matrix products, arithmetic and copies ran while one was open for 7% of the time, Pallas kernels for 0%

commit v1 on v0

--- a/solution.py
+++ b/solution.py
@@ -7,6 +7,22 @@
 HEAD = 64
 EPS = 1e-05
 NEG = -1e30
+
+
+def collect(x, axis, dim):
+    ways, here, hop = (lax.axis_size(axis), lax.axis_index(axis), x.shape[dim])
+    lengths = [n * ways if d == dim else n for d, n in enumerate(x.shape)]
+    full = lax.dynamic_update_slice_in_dim(jnp.zeros(lengths, x.dtype), x, here * hop, axis=dim)
+    going_up = going_down = x
+    for far in range(1, ways // 2 + 1):
+        going_up = lax.ppermute(going_up, axis, [(d, (d + 1) % ways) for d in range(ways)])
+        full = lax.dynamic_update_slice_in_dim(full, going_up, (here - far) % ways * hop, axis=dim)
+        if 2 * far < ways:
+            going_down = lax.ppermute(going_down, axis, [(d, (d - 1) % ways) for d in range(ways)])
+            full = lax.dynamic_update_slice_in_dim(
+                full, going_down, (here + far) % ways * hop, axis=dim
+            )
+    return full
 
 
 def passed_along(value, axis, steps):
@@ -107,7 +123,7 @@
         queries = projected[:, :, 0]
         key_value = projected[:, :, 1:]
         gathered_video, gathered_text = (
-            lax.all_gather(key_value[:, :per_dev], "seq", axis=1, tiled=True),
+            collect(key_value[:, :per_dev], "seq", 1),
             lax.all_gather(key_value[:, per_dev:], "seq", axis=1, tiled=True),
         )
         current = patch_ids == patch_now

time: 723 us -> 889 us (1.23)
  starting transfers between devices: 17.5 us -> 190 us
  blocking collectives: 203 us -> 99 us
  local copies, waits for them, and re-layouts: 116 us -> 163 us
  waiting for transfers between devices: 246 us -> 289 us
    ppermute x0 -> x75, starting transfers between devices: none -> 172 us  [the longest x35 160 us: collect(): lax.ppermute(going_down, axis, [(d, (d - 1) % ways) for d in range(ways)])]
    all_gather x5 -> x0, blocking collectives: 94.4 us -> none  [body(): lax.all_gather(key_value[:, :per_dev], 'seq', axis=1, tiled=True)]
    dynamic_update_slice x0 -> x80, local copies, waits for them, and re-layouts: none -> 50.7 us  [the longest x45 29.8 us: collect(): lax.dynamic_update_slice_in_dim(full, going_up, (here - far) % ways * hop...]
    ppermute x0 -> x75, waiting for transfers between devices: none -> 42.4 us  [the longest x40 42.3 us: collect(): lax.ppermute(going_up, axis, [(d, (d + 1) % ways) for d in range(ways)])]
    all_gather x5, blocking collectives: 103 us -> 92.6 us  [body(): lax.all_gather(key_value[:, per_dev:], 'seq', axis=1, tiled=True)]
    unnamed x117 -> x147, local copies, waits for them, and re-layouts: 41 us -> 43.7 us
    broadcast_in_dim x15 -> x20, local copies, waits for them, and re-layouts: 47 us -> 44.9 us  [body(): jnp.where(current[None, :, None, None, None], gathered_video[:, None], fr...]
  transfers between devices with their start and end apart: 10 -> 85, of which waited for: 9 -> 36; matrix products, arithmetic and copies ran while one was open for 7% -> 13% of each run, Pallas kernels for 0% -> 0%
where the time goes in v1:
time: 889 us; the launch traced here: 878 us
  waiting for transfers between devices  289 us (33%)
  starting transfers between devices  190 us (21%)
  local copies, waits for them, and re-layouts  163 us (18%)
  blocking collectives  99 us (11%)
  matrix products  86.2 us (10%)
  other arithmetic  34.9 us (4%)
  between operations  16.7 us (2%)
    psum x5, waiting for transfers between devices, body(): summed = lax.psum(partial_out, 'mp')  231 us
    ppermute x35, starting transfers between devices, collect(): lax.ppermute(going_down, axis, [(d, (d - 1) % ways) for d in range(ways)])  160 us
    all_gather x5, blocking collectives, body(): lax.all_gather(key_value[:, per_dev:], 'seq', axis=1, tiled=True)  92.6 us
    dot_general x5, matrix products, body(): jnp.dot(normed.reshape(-1, model_width), weight_qkv, preferred_element_ty...  46.6 us
    broadcast_in_dim x20, local copies, waits for them, and re-layouts, body(): jnp.where(current[None, :, None, None, None], gathered_video[:, None], fr...  44.9 us
    unnamed x147, local copies, waits for them, and re-layouts  43.7 us
    ppermute x40, waiting for transfers between devices, collect(): lax.ppermute(going_up, axis, [(d, (d + 1) % ways) for d in range(ways)])  42.3 us
    dynamic_update_slice x45, local copies, waits for them, and re-layouts, collect(): lax.dynamic_update_slice_in_dim(full, going_up, (here - far) % ways * hop...  29.8 us
  transfers between devices with their start and end apart: 85, of which 36 were waited for; matrix products, arithmetic and copies ran while one was open for 13% of the time, Pallas kernels for 0%

profile of v1, /device:TPU:1, one launch (start us, length us, event | category | flops | bytes accessed | tf_op | source)
XLA Modules:
  0.0 877.9 jit_solution(17006821328478828570)
XLA Ops:
  8.0 18.7 %copy.75 = bf16[1,3072,3,768]{1,3,2,0:T(8,128)(2,1)} copy(bf16[1,3072,3,768]{3,1,2,0:T(8,128)(2,1)} %param.15) | data formatting | bytes 28311552 | tf_op args[6]
  27.9 6.4 all-gather.1
  35.5 9.3 %fusion.26 = bf16[2,16,3,768]{3,1,2,0:T(8,128)(2,1)S(1)} fusion(bf16[1,3072,3,768]{1,3,2,0:T(8,128)(2,1)} %copy.75, f32[3072]{0:T(1024)S(1)} %get-tuple-element.81, f32[3072]{0:T(1024)S(1)} %get-tuple-element.82, f32[2,16]{1,0:T(2,128)S(1)} %add_rsqrt_fusion.4, f32[2,16]{1,0:T(2,128)S(1)} %broadcast_multiply_fusion.4, ...), kind=kOutput, calls=%fused_computation.57 | convolution fusion | flops 454139904 | bytes 14524673 | tf_op jit(solution)/shard_map/dot_general | solution.py:119
  46.4 5.0 collective-permute-start.1
  51.5 19.9 %all_gather.22 = bf16[2,128,2,768]{3,1,2,0:T(8,128)(2,1)S(1)} all-gather(bf16[2,8,2,768]{3,1,2,0:T(8,128)(2,1)S(1)} %get-tuple-element.77), channel_id=1, replica_groups=mesh['section'=2,'seq'=16,'mp'=4] {'seq'}, dimensions={1}, use_global_device_ids=true | all-gather | bytes 835584 | tf_op jit(solution)/shard_map/all_gather | solution.py:127
  80.2 4.8 collective-permute-start.5
  86.5 4.8 collective-permute-start.7
  93.5 4.8 collective-permute-start.9
  99.8 4.8 collective-permute-start.11
  106.0 4.8 collective-permute-start.13
  112.8 6.2 collective-permute-done.14
  121.9 5.7 broadcast_in_dim.475
  133.2 9.3 %fusion.259 = (bf16[2,512,1,768]{3,2,1,0:T(2,128)(2,1)}, bf16[2,512,1,768]{3,2,1,0:T(2,128)(2,1)}) fusion(bf16[2,512,2,768]{3,2,1,0:T(2,128)(2,1)} %bitcast.353), kind=kLoop, calls=%fused_computation.463 | loop fusion | bytes 6291456 | tf_op jit(solution)/shard_map/slice | solution.py:52
  142.5 6.8 copy.115
  149.3 8.1 copy.114
  165.5 45.3 %all-reduce.7.cloned.1.call-done = f32[2,16,3072]{2,1,0:T(8,128)} async-done(((f32[2,16,3072]{2,1,0:T(8,128)}), f32[2,16,3072]{2,1,0:T(8,128)}) %all-reduce.7.cloned.1.call-update) | async-done | bytes 393232 | tf_op jit(solution)/shard_map/psum | solution.py:160
  211.8 4.3 collective-permute-start.15
  220.6 9.3 %fusion.29 = bf16[2,16,3,768]{3,1,2,0:T(8,128)(2,1)S(1)} fusion(bf16[1,3072,3,768]{1,3,2,0:T(8,128)(2,1)} %copy.75, bf16[2,16,3072]{2,1,0:T(8,128)(2,1)S(1)} %get-tuple-element.37, f32[2,16]{1,0:T(2,128)S(1)} %add_rsqrt_fusion.3, f32[2,16]{1,0:T(2,128)S(1)} %broadcast_multiply_fusion.3, f32[3072]{0:T(1024)S(1)} %get-tuple-element.81, ...), kind=kOutput, calls=%fused_computation.58 | convolution fusion | flops 453648384 | bytes 14524672 | tf_op jit(solution)/shard_map/dot_general | solution.py:119
  236.4 18.0 %all_gather.24 = bf16[2,128,2,768]{3,1,2,0:T(8,128)(2,1)S(1)} all-gather(bf16[2,8,2,768]{3,1,2,0:T(8,128)(2,1)} %get-tuple-element.74), channel_id=1, replica_groups=mesh['section'=2,'seq'=16,'mp'=4] {'seq'}, dimensions={1}, use_global_device_ids=true | all-gather | bytes 835584 | tf_op jit(solution)/shard_map/all_gather | solution.py:127
  261.1 4.0 collective-permute-start.19
  267.2 4.8 collective-permute-start.21
  274.3 4.8 collective-permute-start.23
  280.6 4.8 collective-permute-start.25
  286.8 4.8 collective-permute-start.27
  293.1 4.8 collective-permute-start.29
  300.0 5.0 collective-permute-done.30
  309.6 5.7 broadcast_in_dim.487
  327.1 47.7 %all-reduce.9.cloned.1.call-done = f32[2,16,3072]{2,1,0:T(8,128)} async-done(((f32[2,16,3072]{2,1,0:T(8,128)}), f32[2,16,3072]{2,1,0:T(8,128)}) %all-reduce.9.cloned.1.call-update) | async-done | bytes 393232 | tf_op jit(solution)/shard_map/psum | solution.py:160
  375.9 4.5 collective-permute-start.31
  384.7 9.3 %fusion.32 = bf16[2,16,3,768]{3,1,2,0:T(8,128)(2,1)S(1)} fusion(bf16[1,3072,3,768]{1,3,2,0:T(8,128)(2,1)} %copy.75, bf16[2,16,3072]{2,1,0:T(8,128)(2,1)S(1)} %get-tuple-element.32, f32[2,16]{1,0:T(2,128)S(1)} %add_rsqrt_fusion.2, f32[2,16]{1,0:T(2,128)S(1)} %broadcast_multiply_fusion.2, f32[3072]{0:T(1024)S(1)} %get-tuple-element.81, ...), kind=kOutput, calls=%fused_computation.59 | convolution fusion | flops 453648384 | bytes 14524672 | tf_op jit(solution)/shard_map/dot_general | solution.py:119
  400.7 18.1 %all_gather.25 = bf16[2,128,2,768]{3,1,2,0:T(8,128)(2,1)S(1)} all-gather(bf16[2,8,2,768]{3,1,2,0:T(8,128)(2,1)S(1)} %get-tuple-element.71), channel_id=1, replica_groups=mesh['section'=2,'seq'=16,'mp'=4] {'seq'}, dimensions={1}, use_global_device_ids=true | all-gather | bytes 835584 | tf_op jit(solution)/shard_map/all_gather | solution.py:127
  431.9 4.8 collective-permute-start.37
  439.0 4.8 collective-permute-start.39
  445.2 4.8 collective-permute-start.41
  451.5 4.8 collective-permute-start.43
  457.8 4.8 collective-permute-start.45
  465.0 5.0 collective-permute-done.46
  474.7 5.7 broadcast_in_dim.494
  492.1 47.6 %all-reduce.11.cloned.1.call-done = f32[2,16,3072]{2,1,0:T(8,128)} async-done(((f32[2,16,3072]{2,1,0:T(8,128)}), f32[2,16,3072]{2,1,0:T(8,128)}) %all-reduce.11.cloned.1.call-update) | async-done | bytes 393232 | tf_op jit(solution)/shard_map/psum | solution.py:160
  540.8 4.3 collective-permute-start.47
  545.2 4.0 collective-permute-done.47
  549.6 9.3 %fusion.35 = bf16[2,16,3,768]{3,1,2,0:T(8,128)(2,1)S(1)} fusion(bf16[1,3072,3,768]{1,3,2,0:T(8,128)(2,1)} %copy.75, bf16[2,16,3072]{2,1,0:T(8,128)(2,1)S(1)} %get-tuple-element.27, f32[2,16]{1,0:T(2,128)S(1)} %add_rsqrt_fusion.1, f32[2,16]{1,0:T(2,128)S(1)} %broadcast_multiply_fusion.1, f32[3072]{0:T(1024)S(1)} %get-tuple-element.81, ...), kind=kOutput, calls=%fused_computation.60 | convolution fusion | flops 453648384 | bytes 14524672 | tf_op jit(solution)/shard_map/dot_general | solution.py:119
  565.5 18.0 %all_gather.26 = bf16[2,128,2,768]{3,1,2,0:T(8,128)(2,1)S(1)} all-gather(bf16[2,8,2,768]{3,1,2,0:T(8,128)(2,1)} %get-tuple-element.68), channel_id=1, replica_groups=mesh['section'=2,'seq'=16,'mp'=4] {'seq'}, dimensions={1}, use_global_device_ids=true | all-gather | bytes 835584 | tf_op jit(solution)/shard_map/all_gather | solution.py:127
  590.0 4.0 collective-permute-start.51
  596.1 4.8 collective-permute-start.53
  603.2 5.0 collective-permute-start.55
  609.4 5.0 collective-permute-start.57
  615.7 5.0 collective-permute-start.59
  621.9 5.0 collective-permute-start.61
  628.8 5.0 collective-permute-done.62
  638.4 5.7 broadcast_in_dim.501
  655.9 47.8 %all-reduce.13.cloned.1.call-done = f32[2,16,3072]{2,1,0:T(8,128)} async-done(((f32[2,16,3072]{2,1,0:T(8,128)}), f32[2,16,3072]{2,1,0:T(8,128)}) %all-reduce.13.cloned.1.call-update) | async-done | bytes 393232 | tf_op jit(solution)/shard_map/psum | solution.py:160
  704.7 4.3 collective-permute-start.63
  713.5 9.3 %fusion.38 = bf16[2,16,3,768]{3,1,2,0:T(8,128)(2,1)S(1)} fusion(bf16[1,3072,3,768]{1,3,2,0:T(8,128)(2,1)} %copy.75, bf16[2,16,3072]{2,1,0:T(8,128)(2,1)S(1)} %get-tuple-element.22, f32[2,16]{1,0:T(2,128)S(1)} %add_rsqrt_fusion, f32[2,16]{1,0:T(2,128)S(1)} %broadcast_multiply_fusion, f32[3072]{0:T(1024)S(1)} %get-tuple-element.81, ...), kind=kOutput, calls=%fused_computation.61 | convolution fusion | flops 453648384 | bytes 14524672 | tf_op jit(solution)/shard_map/dot_general | solution.py:119
  730.4 18.5 %all_gather.27 = bf16[2,128,2,768]{3,1,2,0:T(8,128)(2,1)S(1)} all-gather(bf16[2,8,2,768]{3,1,2,0:T(8,128)(2,1)S(1)} %get-tuple-element.66), channel_id=1, replica_groups=mesh['section'=2,'seq'=16,'mp'=4] {'seq'}, dimensions={1}, use_global_device_ids=true | all-gather | bytes 835584 | tf_op jit(solution)/shard_map/all_gather | solution.py:127
  761.3 4.8 collective-permute-start.69
  768.4 4.8 collective-permute-start.71
  774.6 4.8 collective-permute-start.73
  780.9 4.8 collective-permute-start.75
  787.2 4.8 collective-permute-start.77
  794.3 5.0 collective-permute-done.78
  803.9 5.7 broadcast_in_dim.508
  816.1 4.2 fusion.10
  825.5 42.6 %all-reduce.15.cloned.1.call-done = f32[2,16,3072]{2,1,0:T(8,128)} async-done(((f32[2,16,3072]{2,1,0:T(8,128)}), f32[2,16,3072]{2,1,0:T(8,128)}) %all-reduce.15.cloned.1.call-update) | async-done | bytes 393232 | tf_op jit(solution)/shard_map/psum | solution.py:160
  (510 shorter events, 227.7 us)
Async XLA Ops:
  7.2 126.0 %all-gather.4.cloned.1.call-start = ((), (), s32[]{:S(2)}) async-start(), calls=%async_computation.5 | async-start | bytes 3342336 | tf_op jit(solution)/shard_map/all_gather | solution.py:99
  7.9 202.8 %all-reduce.7.cloned.1.call-start = ((), (), s32[]{:S(2)}) async-start(), calls=%async_computation | async-start | bytes 786432 | tf_op jit(solution)/shard_map/psum | solution.py:160
  44.9 29.0 %collective-permute-start = (bf16[2,8,2,768]{3,1,2,0:T(8,128)(2,1)S(1)}, bf16[2,8,2,768]{3,1,2,0:T(8,128)(2,1)S(1)}, u32[]{:S(2)}, u32[]{:S(2)}) collective-permute-start(bf16[2,8,2,768]{3,1,2,0:T(8,128)(2,1)S(1)} %get-tuple-element.79), channel_id=1, source_target_pairs={{0,4},{4,8},{8,12},{12,16},{16,20},{20,24},{24,28},{28,32},{32,36}... | collective-permute-start | bytes 147464 | tf_op jit(solution)/shard_map/ppermute | solution.py:18
  46.4 28.4 %collective-permute-start.1 = (bf16[2,8,2,768]{3,1,2,0:T(8,128)(2,1)S(1)}, bf16[2,8,2,768]{3,1,2,0:T(8,128)(2,1)S(1)}, u32[]{:S(2)}, u32[]{:S(2)}) collective-permute-start(bf16[2,8,2,768]{3,1,2,0:T(8,128)(2,1)S(1)} %get-tuple-element.79), channel_id=1, source_target_pairs={{0,60},{4,0},{8,4},{12,8},{16,12},{20,16},{24,20},{28,24},{32,28},... | collective-permute-start | bytes 147464 | tf_op jit(solution)/shard_map/ppermute | solution.py:21
  74.0 6.3 collective-permute-start.2
  80.2 6.3 collective-permute-start.4
  80.2 6.3 collective-permute-start.5
  86.5 7.0 collective-permute-start.6
  86.5 7.0 collective-permute-start.7
  93.5 6.3 collective-permute-start.8
  93.5 6.3 collective-permute-start.9
  99.7 6.3 collective-permute-start.10
  99.8 6.3 collective-permute-start.11
  106.0 6.3 collective-permute-start.12
  106.0 6.8 collective-permute-start.13
  112.3 6.8 collective-permute-start.14
  165.4 209.4 %all-reduce.9.cloned.1.call-start = ((), (), s32[]{:S(2)}) async-start(), calls=%async_computation.1 | async-start | bytes 786432 | tf_op jit(solution)/shard_map/psum | solution.py:160
  211.8 8.4 collective-permute-start.15
  230.7 28.0 %collective-permute-start.16 = (bf16[2,8,2,768]{3,1,2,0:T(8,128)(2,1)}, bf16[2,8,2,768]{3,1,2,0:T(8,128)(2,1)}, u32[]{:S(2)}, u32[]{:S(2)}) collective-permute-start(bf16[2,8,2,768]{3,1,2,0:T(8,128)(2,1)} %get-tuple-element.76), channel_id=1, source_target_pairs={{0,4},{4,8},{8,12},{12,16},{16,20},{20,24},{24,28},{28,32},{32,36}... | collective-permute-start | bytes 147464 | tf_op jit(solution)/shard_map/ppermute | solution.py:18
  231.9 29.2 %collective-permute-start.17 = (bf16[2,8,2,768]{3,1,2,0:T(8,128)(2,1)}, bf16[2,8,2,768]{3,1,2,0:T(8,128)(2,1)}, u32[]{:S(2)}, u32[]{:S(2)}) collective-permute-start(bf16[2,8,2,768]{3,1,2,0:T(8,128)(2,1)} %get-tuple-element.76), channel_id=1, source_target_pairs={{0,60},{4,0},{8,4},{12,8},{16,12},{20,16},{24,20},{28,24},{32,28},... | collective-permute-start | bytes 147464 | tf_op jit(solution)/shard_map/ppermute | solution.py:21
  258.7 7.9 collective-permute-start.18
  266.6 7.1 collective-permute-start.20
  267.2 7.1 collective-permute-start.21
  273.7 6.3 collective-permute-start.22
  274.3 6.3 collective-permute-start.23
  279.9 6.3 collective-permute-start.24
  280.6 6.3 collective-permute-start.25
  286.2 6.3 collective-permute-start.26
  292.4 6.3 collective-permute-start.28
  298.7 6.3 collective-permute-start.30
  327.0 212.8 %all-reduce.11.cloned.1.call-start = ((), (), s32[]{:S(2)}) async-start(), calls=%async_computation.2 | async-start | bytes 786432 | tf_op jit(solution)/shard_map/psum | solution.py:160
  375.9 8.4 collective-permute-start.31
  395.6 28.0 %collective-permute-start.32 = (bf16[2,8,2,768]{3,1,2,0:T(8,128)(2,1)S(1)}, bf16[2,8,2,768]{3,1,2,0:T(8,128)(2,1)}, u32[]{:S(2)}, u32[]{:S(2)}) collective-permute-start(bf16[2,8,2,768]{3,1,2,0:T(8,128)(2,1)S(1)} %get-tuple-element.73), channel_id=1, source_target_pairs={{0,4},{4,8},{8,12},{12,16},{16,20},{20,24},{24,28},{28,32},{32,36}... | collective-permute-start | bytes 147464 | tf_op jit(solution)/shard_map/ppermute | solution.py:18
  396.8 29.4 %collective-permute-start.33 = (bf16[2,8,2,768]{3,1,2,0:T(8,128)(2,1)S(1)}, bf16[2,8,2,768]{3,1,2,0:T(8,128)(2,1)}, u32[]{:S(2)}, u32[]{:S(2)}) collective-permute-start(bf16[2,8,2,768]{3,1,2,0:T(8,128)(2,1)S(1)} %get-tuple-element.73), channel_id=1, source_target_pairs={{0,60},{4,0},{8,4},{12,8},{16,12},{20,16},{24,20},{28,24},{32,28},... | collective-permute-start | bytes 147464 | tf_op jit(solution)/shard_map/ppermute | solution.py:21
  423.6 7.7 collective-permute-start.34
  431.3 7.1 collective-permute-start.36
  431.9 7.1 collective-permute-start.37
  439.0 6.3 collective-permute-start.39
  445.2 6.3 collective-permute-start.41
  450.9 6.3 collective-permute-start.42
  457.8 6.7 collective-permute-start.45
  463.4 6.6 collective-permute-start.46
  492.1 211.6 %all-reduce.13.cloned.1.call-start = ((), (), s32[]{:S(2)}) async-start(), calls=%async_computation.3 | async-start | bytes 786432 | tf_op jit(solution)/shard_map/psum | solution.py:160
  540.8 8.4 collective-permute-start.47
  559.7 28.0 %collective-permute-start.48 = (bf16[2,8,2,768]{3,1,2,0:T(8,128)(2,1)}, bf16[2,8,2,768]{3,1,2,0:T(8,128)(2,1)}, u32[]{:S(2)}, u32[]{:S(2)}) collective-permute-start(bf16[2,8,2,768]{3,1,2,0:T(8,128)(2,1)} %get-tuple-element.70), channel_id=1, source_target_pairs={{0,4},{4,8},{8,12},{12,16},{16,20},{20,24},{24,28},{28,32},{32,36}... | collective-permute-start | bytes 147464 | tf_op jit(solution)/shard_map/ppermute | solution.py:18
  560.9 29.0 %collective-permute-start.49 = (bf16[2,8,2,768]{3,1,2,0:T(8,128)(2,1)}, bf16[2,8,2,768]{3,1,2,0:T(8,128)(2,1)}, u32[]{:S(2)}, u32[]{:S(2)}) collective-permute-start(bf16[2,8,2,768]{3,1,2,0:T(8,128)(2,1)} %get-tuple-element.70), channel_id=1, source_target_pairs={{0,60},{4,0},{8,4},{12,8},{16,12},{20,16},{24,20},{28,24},{32,28},... | collective-permute-start | bytes 147464 | tf_op jit(solution)/shard_map/ppermute | solution.py:21
  587.8 7.7 collective-permute-start.50
  595.5 7.1 collective-permute-start.52
  596.1 7.1 collective-permute-start.53
  602.5 6.3 collective-permute-start.54
  603.2 6.3 collective-permute-start.55
  609.4 6.3 collective-permute-start.57
  615.0 6.3 collective-permute-start.58
  655.8 212.2 %all-reduce.15.cloned.1.call-start = ((), (), s32[]{:S(2)}) async-start(), calls=%async_computation.4 | async-start | bytes 786432 | tf_op jit(solution)/shard_map/psum | solution.py:160
  704.7 8.4 collective-permute-start.63
  725.4 27.6 %collective-permute-start.64 = (bf16[2,8,2,768]{3,1,2,0:T(8,128)(2,1)S(1)}, bf16[2,8,2,768]{3,1,2,0:T(8,128)(2,1)}, u32[]{:S(2)}, u32[]{:S(2)}) collective-permute-start(bf16[2,8,2,768]{3,1,2,0:T(8,128)(2,1)S(1)} %get-tuple-element.67), channel_id=1, source_target_pairs={{0,4},{4,8},{8,12},{12,16},{16,20},{20,24},{24,28},{28,32},{32,36}... | collective-permute-start | bytes 147464 | tf_op jit(solution)/shard_map/ppermute | solution.py:18
  726.6 28.9 %collective-permute-start.65 = (bf16[2,8,2,768]{3,1,2,0:T(8,128)(2,1)S(1)}, bf16[2,8,2,768]{3,1,2,0:T(8,128)(2,1)}, u32[]{:S(2)}, u32[]{:S(2)}) collective-permute-start(bf16[2,8,2,768]{3,1,2,0:T(8,128)(2,1)S(1)} %get-tuple-element.67), channel_id=1, source_target_pairs={{0,60},{4,0},{8,4},{12,8},{16,12},{20,16},{24,20},{28,24},{32,28},... | collective-permute-start | bytes 147464 | tf_op jit(solution)/shard_map/ppermute | solution.py:21
  753.0 7.7 collective-permute-start.66
  760.7 7.1 collective-permute-start.68
  761.3 7.1 collective-permute-start.69
  774.0 6.3 collective-permute-start.72
  780.9 6.3 collective-permute-start.75
  787.2 6.5 collective-permute-start.77
  792.8 6.5 collective-permute-start.78
  (92 other events, 1590.4 us)
Sparse Core Ops, SparseCore 0:
  10.2 51.7 all-gather.3
  165.5 45.1 all-reduce.6
  327.1 47.6 all-reduce.8
  492.2 47.5 all-reduce.10
  655.9 47.6 all-reduce.12
  820.4 47.5 all-reduce.14
